TPU v7x, 32 devices: a whole 2x2x4 slice. The times are simulated.
32 devices in a mesh: row: 4 (over y, core), col: 8 (over z, x).
Axes of the slice: x: 2, y: 2, z: 4, core: 2. Of those that a mesh axis runs over, the one named last changes fastest.
Arguments:
- transfer: bfloat16 [2048, 2, 512, 256], P(('row', 'col')), may hold values from -0.65625 to 0.65625
- target: bfloat16 [2048, 2, 32, 512], P(('row', 'col')), may hold values from -6 to 6
- zone_mask: int32 [32, 512], replicated, may hold values 0 or 1
- dark_weight: float32 [32], replicated, may hold values from 1 to 4
- reg_weight: float32 [2048], P(('row', 'col')), may hold values from 0.05 to 2
- momentum: float32 [1], replicated, may hold values from 0.2 to 0.8
Outputs:
- filters: float32 [32, 256, 1024], P(None, ('row', 'col'))
- residual: float32 [32, 256, 1024], P(None, ('row', 'col'))
All inputs are finite; a program needn't handle non-finite values.
Results may differ from a plain program's by a relative error of at most 0.0059.
Values may be sent and summed in bfloat16 or wider, within the bound.
No kernel may reach another device: no remote copies, remote signals or barrier semaphores. Data moves between devices by JAX's collectives and lax.ppermute only.
A program may use at most 128 MiB of HBM per device.

v0:
```python
import math
import jax
import jax.numpy as jnp
from jax import lax
from jax.sharding import PartitionSpec as P

K = 1024
F = 2048
ITERS = 2


def build_table(taps, bins):
    tap_index = jnp.arange(taps, dtype=jnp.int32)[:, None]
    bin_index = jnp.arange(bins, dtype=jnp.int32)[None, :]
    phase = (tap_index * bin_index % bins).astype(jnp.float32) * (2.0 * math.pi / bins)
    return jnp.stack([jnp.cos(phase), -jnp.sin(phase)], axis=1) / math.sqrt(bins)


def body(transfer, target, zone_mask, dark_weight, reg_weight, momentum):
    dft_table = build_table(K, F)
    mic_gains = jnp.where(zone_mask == 1, jnp.float32(1.0), dark_weight[:, None])
    weight_real = transfer[:, 0]
    weight_imag = transfer[:, 1]
    reg_term = reg_weight[:, None, None]

    def to_taps(spectrum):
        regrouped = lax.all_to_all(
            spectrum, ("row", "col"), split_axis=3, concat_axis=0, tiled=True
        )
        return jnp.einsum("fctl,kcf->tlk", regrouped, dft_table, precision=lax.Precision.HIGHEST)

    def back_project(err_real, err_imag):
        back_real = jnp.einsum(
            "fml,ftm->ftl", weight_real, err_real, preferred_element_type=jnp.float32
        )
        back_real = back_real + jnp.einsum(
            "fml,ftm->ftl", weight_imag, err_imag, preferred_element_type=jnp.float32
        )
        back_imag = jnp.einsum(
            "fml,ftm->ftl", weight_real, err_imag, preferred_element_type=jnp.float32
        )
        back_imag = back_imag - jnp.einsum(
            "fml,ftm->ftl", weight_imag, err_real, preferred_element_type=jnp.float32
        )
        return (back_real, back_imag)

    rhs_error = jnp.where(zone_mask[None, None] == 1, target, jnp.zeros_like(target))
    rhs_real, rhs_imag = back_project(rhs_error[:, 0], rhs_error[:, 1])
    rhs = to_taps(jnp.stack([rhs_real, rhs_imag], axis=1))
    filters = jnp.zeros_like(rhs)
    residual = rhs
    direction = rhs
    for iteration in range(ITERS):
        along_term = jnp.sum(residual * direction)
        to_spectrum = jnp.einsum(
            "tlk,kcf->fctl", direction, dft_table, precision=lax.Precision.HIGHEST
        ).astype(jnp.bfloat16)
        to_regrouped = lax.all_to_all(
            to_spectrum, ("row", "col"), split_axis=0, concat_axis=3, tiled=True
        )
        spec_real = to_regrouped[:, 0]
        spec_imag = to_regrouped[:, 1]
        press_real = jnp.einsum(
            "fml,ftl->ftm", weight_real, spec_real, preferred_element_type=jnp.float32
        )
        press_real = press_real - jnp.einsum(
            "fml,ftl->ftm", weight_imag, spec_imag, preferred_element_type=jnp.float32
        )
        press_imag = jnp.einsum(
            "fml,ftl->ftm", weight_real, spec_imag, preferred_element_type=jnp.float32
        )
        press_imag = press_imag + jnp.einsum(
            "fml,ftl->ftm", weight_imag, spec_real, preferred_element_type=jnp.float32
        )
        weighted_real = mic_gains * press_real
        weighted_imag = mic_gains * press_imag
        operator_back_real, operator_back_imag = back_project(
            weighted_real.astype(jnp.bfloat16), weighted_imag.astype(jnp.bfloat16)
        )
        wide_real = spec_real.astype(jnp.float32)
        wide_imag = spec_imag.astype(jnp.float32)
        totals = None
        combined = jnp.stack(
            [operator_back_real + reg_term * wide_real, operator_back_imag + reg_term * wide_imag],
            axis=1,
        )
        image_taps, totals = (to_taps(combined), totals)
        along_sum, bend_sum = lax.psum(
            (along_term, jnp.sum(direction * image_taps)), ("row", "col")
        )
        step_size = along_sum / bend_sum
        filters = filters + step_size * direction
        residual = residual - step_size * image_taps
        if iteration + 1 < ITERS:
            direction = residual + momentum[iteration] * direction
    return (filters, residual)


def solution(mesh):
    in_specs = (
        P(("row", "col"), None, None, None),
        P(("row", "col"), None, None, None),
        P(),
        P(),
        P(("row", "col")),
        P(),
    )
    out_specs = (P(None, ("row", "col"), None), P(None, ("row", "col"), None))
    return jax.shard_map(body, mesh=mesh, in_specs=in_specs, out_specs=out_specs, check_vma=False)
```

profile of v0, /device:TPU:0, one launch (start us, length us, event | category | flops | bytes accessed | tf_op | source)
XLA Modules:
  0.0 1125.6 jit_solution(2938262932582563198)
XLA Ops:
  62.3 34.6 %sine_negate_fusion = (f32[1024,1,2048]{2,0,1:T(8,128)}, f32[1024,1,2048]{2,0,1:T(8,128)}) fusion(), kind=kLoop, calls=%fused_computation.57 | loop fusion | flops 31457280 | bytes 16777216 | tf_op jit(solution)/shard_map/neg | solution.py:16
  96.8 60.6 %all-to-all-done = f32[32,1,32768]{2,1,0:T(1,128)} async-done(((f32[32,1,32768]{2,1,0:T(1,128)}), f32[32,1,32768]{2,1,0:T(1,128)}, u32[]{:S(2)}, u32[]{:S(2)}) %all-to-all-start) | async-done | bytes 4194336 | tf_op jit(solution)/shard_map/all_to_all | solution.py:27
  158.0 13.8 %reduce = f32[32,32768]{1,0:T(8,128)} reduce(f32[32,1,32768]{2,1,0:T(1,128)} %all-to-all-done, f32[]{:T(128)} %broadcast.90), dimensions={1}, to_apply=%all_to_all.65.reduce_sub_computation | reduce | bytes 8388612 | tf_op jit(solution)/shard_map/all_to_all | solution.py:27
  198.4 18.7 %fusion.81 = f32[32,8,1024]{2,1,0:T(8,128)S(1)} fusion(f32[2048,2,32,8]{0,3,1,2:T(8,128)} %all_to_all.68, f32[1024,1,2048]{2,0,1:T(8,128)} %get-tuple-element.20, f32[1024,1,2048]{2,0,1:T(8,128)} %get-tuple-element.21), kind=kOutput, calls=%fused_computation.90 | convolution fusion | flops 12893290496 | bytes 22020096 | tf_op jit(solution)/shard_map/fctl,kcf->tlk/dot_general | solution.py:30
  218.0 19.9 %fusion.66 = bf16[2048,2,32,8]{0,2,3,1:T(8,128)(2,1)S(1)} fusion(f32[32,8,1024]{2,1,0:T(8,128)S(1)} %fusion.81, f32[1024,1,2048]{2,0,1:T(8,128)} %get-tuple-element.20, f32[1024,1,2048]{2,0,1:T(8,128)} %get-tuple-element.21), kind=kOutput, calls=%fused_computation.73 | convolution fusion | flops 12894339072 | bytes 19922944 | tf_op jit(solution)/shard_map/tlk,kcf->fctl/dot_general | solution.py:55
  246.5 12.2 %reshape.86 = bf16[32,2,16384]{2,1,0:T(2,128)(2,1)S(1)} reshape(bf16[2048,2,8,32]{3,2,1,0:T(8,128)(2,1)} %bitcast.200) | data formatting | bytes 4194304
  258.8 52.7 %all_to_all.90 = bf16[32,2,16384]{2,1,0:T(2,128)(2,1)} all-to-all(bf16[32,2,16384]{2,1,0:T(2,128)(2,1)S(1)} %reshape.86), channel_id=1, replica_groups=mesh['row'=4,'col'=8] {'row','col'}, dimensions={0} | all-to-all | bytes 4194304 | tf_op jit(solution)/shard_map/all_to_all | solution.py:58
  323.2 12.1 %copy.65 = bf16[32,64,2,32,8]{1,4,0,3,2:T(8,128)(2,1)} copy(bf16[32,64,2,32,8]{3,4,2,1,0:T(8,128)(2,1)} %bitcast.201) | data formatting | bytes 4194304 | tf_op jit(solution)/shard_map/all_to_all | solution.py:58
  342.7 12.7 %fusion.12 = f32[64,32,512]{2,1,0:T(8,128)} fusion(bf16[64,1,32,256]{3,2,0,1:T(8,128)(2,1)S(1)} %copy.88, bf16[64,2,512,256]{3,2,1,0:T(8,128)(2,1)} %param.6), kind=kOutput, calls=%fused_computation.13 | convolution fusion | flops 536870912 | bytes 22020096 | tf_op jit(solution)/shard_map/fml,ftl->ftm/dot_general | solution.py:72
  355.4 12.7 %fusion.34 = f32[64,32,512]{2,1,0:T(8,128)} fusion(bf16[64,1,32,256]{3,2,0,1:T(8,128)(2,1)S(1)} %copy.88, bf16[64,2,512,256]{3,2,1,0:T(8,128)(2,1)} %param.6), kind=kOutput, calls=%fused_computation.35 | convolution fusion | flops 536870912 | bytes 22020096 | tf_op jit(solution)/shard_map/fml,ftl->ftm/dot_general | solution.py:63
  371.2 12.7 %fusion.30 = f32[64,32,512]{2,1,0:T(8,128)} fusion(bf16[64,1,32,256]{3,2,0,1:T(8,128)(2,1)S(1)} %copy.89, bf16[64,2,512,256]{3,2,1,0:T(8,128)(2,1)} %param.6), kind=kOutput, calls=%fused_computation.31 | convolution fusion | flops 536870912 | bytes 22020096 | tf_op jit(solution)/shard_map/fml,ftl->ftm/dot_general | solution.py:69
  383.9 12.7 %fusion.14 = f32[64,32,512]{2,1,0:T(8,128)} fusion(bf16[64,1,32,256]{3,2,0,1:T(8,128)(2,1)S(1)} %copy.89, bf16[64,2,512,256]{3,2,1,0:T(8,128)(2,1)} %param.6), kind=kOutput, calls=%fused_computation.15 | convolution fusion | flops 536870912 | bytes 22020096 | tf_op jit(solution)/shard_map/fml,ftl->ftm/dot_general | solution.py:66
  420.4 12.8 %add_bitcast_fusion.3 = f32[64,1,32,256]{3,2,0,1:T(8,128)} fusion(f32[64,32,256]{2,1,0:T(8,128)} %fusion.10, f32[64,32,512]{2,1,0:T(8,128)} %fusion.34, f32[64,32,512]{2,1,0:T(8,128)} %fusion.14, f32[32,512]{1,0:T(8,128)S(1)} %get-tuple-element.10, bf16[64,1,32,256]{3,2,0,1:T(8,128)(2,1)S(1)} %copy.88, f32[64]{0:T(128)S(1)} %copy-done.9, ...), kind=kOutput, calls=%fused_computation.79 | convolution fusion | flops 542113792 | bytes 30474496 | tf_op jit(solution)/shard_map/fml,ftm->ftl/dot_general | solution.py:33
  433.3 13.1 %add_bitcast_fusion.2 = f32[64,1,32,256]{3,2,0,1:T(8,128)} fusion(f32[64,32,256]{2,1,0:T(8,128)} %fusion.8, f32[64,32,512]{2,1,0:T(8,128)} %fusion.30, f32[64,32,512]{2,1,0:T(8,128)} %fusion.12, f32[32,512]{1,0:T(8,128)S(1)} %get-tuple-element.10, bf16[64,1,32,256]{3,2,0,1:T(8,128)(2,1)S(1)} %copy.89, f32[64]{0:T(128)S(1)} %copy-done.9, ...), kind=kOutput, calls=%fused_computation.78 | convolution fusion | flops 542113792 | bytes 30474496 | tf_op jit(solution)/shard_map/fml,ftm->ftl/dot_general | solution.py:39
  473.6 94.5 %all-to-all-done.2 = f32[32,1,32768]{2,1,0:T(1,128)} async-done(((f32[32,1,32768]{2,1,0:T(1,128)}), f32[32,1,32768]{2,1,0:T(1,128)}, u32[]{:S(2)}, u32[]{:S(2)}) %all-to-all-start.2) | async-done | bytes 4194336 | tf_op jit(solution)/shard_map/all_to_all | solution.py:27
  568.1 13.8 %reduce.1 = f32[32,32768]{1,0:T(8,128)} reduce(f32[32,1,32768]{2,1,0:T(1,128)} %all-to-all-done.2, f32[]{:T(128)} %broadcast.90), dimensions={1}, to_apply=%all_to_all.73.reduce_sub_computation | reduce | bytes 8388612 | tf_op jit(solution)/shard_map/all_to_all | solution.py:27
  608.5 19.5 %multiply_reduce_fusion.2 = (f32[]{:T(128)}, f32[]{:T(128)}, f32[32,8,1024]{2,1,0:T(8,128)S(1)}) fusion(f32[32,8,1024]{2,1,0:T(8,128)S(1)} %copy-done.3, f32[2048,2,32,8]{0,3,1,2:T(8,128)} %all_to_all.76, f32[1024,1,2048]{2,0,1:T(8,128)} %get-tuple-element.20, f32[1024,1,2048]{2,0,1:T(8,128)} %get-tuple-element.21), kind=kOutput, calls=%fused_computation.111 | convolution fusion | flops 12894339072 | bytes 23068680 | tf_op jit(solution)/shard_map/fctl,kcf->tlk/dot_general | solution.py:30
  628.1 37.4 %all-reduce.1 = (f32[]{:T(128)}, f32[]{:T(128)}) all-reduce(f32[]{:T(128)} %get-tuple-element.5, f32[]{:T(128)} %get-tuple-element.4), channel_id=1, replica_groups=mesh['row'=4,'col'=8] {'row','col'}, use_global_device_ids=true, to_apply=%region_1.2 | all-reduce | flops 2 | bytes 16 | tf_op jit(solution)/shard_map/psum | solution.py:88
  667.1 21.2 %fusion.63 = bf16[2048,2,32,8]{0,2,3,1:T(8,128)(2,1)} fusion(f32[32,8,1024]{2,1,0:T(8,128)S(1)} %multiply_add_fusion.1, f32[1024,1,2048]{2,0,1:T(8,128)} %get-tuple-element.20, f32[1024,1,2048]{2,0,1:T(8,128)} %get-tuple-element.21), kind=kOutput, calls=%fused_computation.72 | convolution fusion | flops 12894339072 | bytes 19922944 | tf_op jit(solution)/shard_map/tlk,kcf->fctl/dot_general | solution.py:55
  698.3 12.2 %reshape.90 = bf16[32,2,16384]{2,1,0:T(2,128)(2,1)S(1)} reshape(bf16[2048,2,8,32]{3,2,1,0:T(8,128)(2,1)} %bitcast.202) | data formatting | bytes 4194304
  710.5 55.8 %all_to_all.91 = bf16[32,2,16384]{2,1,0:T(2,128)(2,1)} all-to-all(bf16[32,2,16384]{2,1,0:T(2,128)(2,1)S(1)} %reshape.90), channel_id=1, replica_groups=mesh['row'=4,'col'=8] {'row','col'}, dimensions={0} | all-to-all | bytes 4194304 | tf_op jit(solution)/shard_map/all_to_all | solution.py:58
  778.0 12.1 %copy.73 = bf16[32,64,2,32,8]{1,4,0,3,2:T(8,128)(2,1)} copy(bf16[32,64,2,32,8]{3,4,2,1,0:T(8,128)(2,1)} %bitcast.203) | data formatting | bytes 4194304 | tf_op jit(solution)/shard_map/all_to_all | solution.py:58
  797.5 12.7 %fusion.4 = f32[64,32,512]{2,1,0:T(8,128)} fusion(bf16[64,1,32,256]{3,2,0,1:T(8,128)(2,1)S(1)} %copy.90, bf16[64,2,512,256]{3,2,1,0:T(8,128)(2,1)} %param.6), kind=kOutput, calls=%fused_computation.5 | convolution fusion | flops 536870912 | bytes 22020096 | tf_op jit(solution)/shard_map/fml,ftl->ftm/dot_general | solution.py:72
  810.2 12.7 %fusion.26 = f32[64,32,512]{2,1,0:T(8,128)} fusion(bf16[64,1,32,256]{3,2,0,1:T(8,128)(2,1)S(1)} %copy.90, bf16[64,2,512,256]{3,2,1,0:T(8,128)(2,1)} %param.6), kind=kOutput, calls=%fused_computation.27 | convolution fusion | flops 536870912 | bytes 22020096 | tf_op jit(solution)/shard_map/fml,ftl->ftm/dot_general | solution.py:63
  825.8 12.7 %fusion.22 = f32[64,32,512]{2,1,0:T(8,128)} fusion(bf16[64,1,32,256]{3,2,0,1:T(8,128)(2,1)S(1)} %copy.91, bf16[64,2,512,256]{3,2,1,0:T(8,128)(2,1)} %param.6), kind=kOutput, calls=%fused_computation.23 | convolution fusion | flops 536870912 | bytes 22020096 | tf_op jit(solution)/shard_map/fml,ftl->ftm/dot_general | solution.py:69
  838.5 12.7 %fusion.6 = f32[64,32,512]{2,1,0:T(8,128)} fusion(bf16[64,1,32,256]{3,2,0,1:T(8,128)(2,1)S(1)} %copy.91, bf16[64,2,512,256]{3,2,1,0:T(8,128)(2,1)} %param.6), kind=kOutput, calls=%fused_computation.7 | convolution fusion | flops 536870912 | bytes 22020096 | tf_op jit(solution)/shard_map/fml,ftl->ftm/dot_general | solution.py:66
  875.0 12.8 %add_bitcast_fusion.1 = f32[64,1,32,256]{3,2,0,1:T(8,128)} fusion(f32[64,32,256]{2,1,0:T(8,128)} %fusion.2, f32[64,32,512]{2,1,0:T(8,128)} %fusion.26, f32[64,32,512]{2,1,0:T(8,128)} %fusion.6, f32[32,512]{1,0:T(8,128)S(1)} %get-tuple-element.10, bf16[64,1,32,256]{3,2,0,1:T(8,128)(2,1)S(1)} %copy.90, f32[64]{0:T(128)S(1)} %copy-done.9, ...), kind=kOutput, calls=%fused_computation.77 | convolution fusion | flops 542113792 | bytes 30474496 | tf_op jit(solution)/shard_map/fml,ftm->ftl/dot_general | solution.py:33
  887.9 13.1 %add_bitcast_fusion = f32[64,1,32,256]{3,2,0,1:T(8,128)} fusion(f32[64,32,256]{2,1,0:T(8,128)} %fusion, f32[64,32,512]{2,1,0:T(8,128)} %fusion.22, f32[64,32,512]{2,1,0:T(8,128)} %fusion.4, f32[32,512]{1,0:T(8,128)S(1)} %get-tuple-element.10, bf16[64,1,32,256]{3,2,0,1:T(8,128)(2,1)S(1)} %copy.91, f32[64]{0:T(128)S(1)} %copy-done.9, ...), kind=kOutput, calls=%fused_computation.76 | convolution fusion | flops 542113792 | bytes 30474496 | tf_op jit(solution)/shard_map/fml,ftm->ftl/dot_general | solution.py:39
  924.0 98.5 %all_to_all.92 = f32[32,1,32768]{2,1,0:T(1,128)} all-to-all(f32[32,1,32768]{2,1,0:T(1,128)} %reshape.92), channel_id=1, replica_groups=mesh['row'=4,'col'=8] {'row','col'}, dimensions={0} | all-to-all | bytes 8388608 | tf_op jit(solution)/shard_map/all_to_all | solution.py:27
  1022.5 13.8 %reduce.2 = f32[32,32768]{1,0:T(8,128)} reduce(f32[32,1,32768]{2,1,0:T(1,128)} %all_to_all.92, f32[]{:T(128)} %broadcast.90), dimensions={1}, to_apply=%all_to_all.81.reduce_sub_computation | reduce | bytes 8388612 | tf_op jit(solution)/shard_map/all_to_all | solution.py:27
  1063.1 19.6 %multiply_reduce_fusion = (f32[]{:T(128)}, f32[]{:T(128)}, f32[32,8,1024]{2,1,0:T(8,128)}) fusion(f32[32,8,1024]{2,1,0:T(8,128)S(1)} %copy-done.8, f32[32,8,1024]{2,1,0:T(8,128)S(1)} %copy-done.4, f32[32,8,1024]{2,1,0:T(8,128)S(1)} %copy-done.6, f32[]{:T(128)S(6)} %div.14, f32[2048,2,32,8]{0,3,1,2:T(8,128)} %all_to_all.84, ...), kind=kOutput, calls=%fused_computation.107 | convolution fusion | flops 12894863360 | bytes 25165836 | tf_op jit(solution)/shard_map/fctl,kcf->tlk/dot_general | solution.py:30
  1082.7 38.0 %all-reduce = (f32[]{:T(128)}, f32[]{:T(128)}) all-reduce(f32[]{:T(128)} %get-tuple-element.3, f32[]{:T(128)} %get-tuple-element.2), channel_id=1, replica_groups=mesh['row'=4,'col'=8] {'row','col'}, use_global_device_ids=true, to_apply=%region_5.6 | all-reduce | flops 2 | bytes 16 | tf_op jit(solution)/shard_map/psum | solution.py:88
  (63 shorter events, 306.5 us)
Async XLA Ops:
  54.3 103.1 %all-to-all-start = ((f32[32,1,32768]{2,1,0:T(1,128)}), f32[32,1,32768]{2,1,0:T(1,128)}, u32[]{:S(2)}, u32[]{:S(2)}) async-start(f32[32,1,32768]{2,1,0:T(1,128)} %reshape.84), calls=%async_computation | async-start | bytes 8388608 | tf_op jit(solution)/shard_map/all_to_all | solution.py:27
  217.1 1.0 copy-start.2
  408.5 11.9 %copy-start.9 = (f32[64]{0:T(128)S(1)}, f32[64]{0:T(128)}, u32[]{:S(2)}) copy-start(f32[64]{0:T(128)} %param.10) | copy-start | bytes 772
  433.2 13.1 %copy-start.1 = (f32[64,1,32,256]{3,2,0,1:T(8,128)S(1)}, f32[64,1,32,256]{3,2,0,1:T(8,128)}, u32[]{:S(2)}) copy-start(f32[64,1,32,256]{3,2,0,1:T(8,128)} %add_bitcast_fusion.3) | copy-start | bytes 6291460
  469.3 98.7 %all-to-all-start.2 = ((f32[32,1,32768]{2,1,0:T(1,128)}), f32[32,1,32768]{2,1,0:T(1,128)}, u32[]{:S(2)}, u32[]{:S(2)}) async-start(f32[32,1,32768]{2,1,0:T(1,128)} %reshape.88), calls=%async_computation.2 | async-start | bytes 8388608 | tf_op jit(solution)/shard_map/all_to_all | solution.py:27
  600.6 7.9 copy-start.3
  628.1 60.2 %copy-start.5 = (f32[32,8,1024]{2,1,0:T(8,128)}, f32[32,8,1024]{2,1,0:T(8,128)S(1)}, u32[]{:S(2)}) copy-start(f32[32,8,1024]{2,1,0:T(8,128)S(1)} %get-tuple-element.18) | copy-start | bytes 3145732
  667.1 21.2 %copy-start.7 = (f32[32,8,1024]{2,1,0:T(8,128)}, f32[32,8,1024]{2,1,0:T(8,128)S(1)}, u32[]{:S(2)}) copy-start(f32[32,8,1024]{2,1,0:T(8,128)S(1)} %multiply_add_fusion.1) | copy-start | bytes 3145732
  887.9 13.1 %copy-start = (f32[64,1,32,256]{3,2,0,1:T(8,128)S(1)}, f32[64,1,32,256]{3,2,0,1:T(8,128)}, u32[]{:S(2)}) copy-start(f32[64,1,32,256]{3,2,0,1:T(8,128)} %add_bitcast_fusion.1) | copy-start | bytes 6291460
  1055.1 8.0 copy-start.4
  1055.1 8.0 copy-start.6
  1055.1 8.0 copy-start.8
where the time goes:
time: 1140 us; the launch traced here: 1130 us
  matrix products  329 us (29%)
  blocking collectives  283 us (25%)
  local copies, waits for them, and re-layouts  250 us (22%)
  waiting for transfers between devices  155 us (14%)
  other arithmetic  93.1 us (8%)
  starting transfers between devices  11.5 us (1%)
    all_to_all x2, waiting for transfers between devices, to_taps(): lax.all_to_all(spectrum, ('row', 'col'), split_axis=3, concat_axis=0, til...  155 us
    unnamed x34, local copies, waits for them, and re-layouts  112 us
    all_to_all x2, blocking collectives, body(): lax.all_to_all(to_spectrum, ('row', 'col'), split_axis=0, concat_axis=3,...  109 us
    all_to_all x1, blocking collectives, to_taps(): lax.all_to_all(spectrum, ('row', 'col'), split_axis=3, concat_axis=0, til...  98.5 us
    psum x2, blocking collectives, body(): lax.psum((along_term, jnp.sum(direction * image_taps)), ('row', 'col'))  75.5 us
    all_to_all x7, local copies, waits for them, and re-layouts, to_taps(): lax.all_to_all(spectrum, ('row', 'col'), split_axis=3, concat_axis=0, til...  58.6 us
    dot_general x3, matrix products, to_taps(): jnp.einsum('fctl,kcf->tlk', regrouped, dft_table, precision=lax.Precision...  57.9 us
    all_to_all x3, other arithmetic, to_taps(): lax.all_to_all(spectrum, ('row', 'col'), split_axis=3, concat_axis=0, til...  41.3 us
  transfers between devices with their start and end apart: 2, of which 2 were waited for; matrix products, arithmetic and copies ran while one was open for 3% of the time, Pallas kernels for 0%

commit v1 on v0

--- a/solution.py
+++ b/solution.py
@@ -3,10 +3,20 @@
 import jax.numpy as jnp
 from jax import lax
 from jax.sharding import PartitionSpec as P
+from jax.lax import all_to_all, axis_size
 
 K = 1024
 F = 2048
 ITERS = 2
+
+
+def plan_the_gates(field):
+    w1 = axis_size(("row", "col"))
+    x_next = jnp.split(field, w1, 0)
+    block_next = jnp.stack(x_next, axis=0)
+    newest = all_to_all(block_next, ("row", "col"), 0, 0)
+    view_out = jnp.concatenate(newest, axis=3)
+    return view_out
 
 
 def build_table(taps, bins):
@@ -55,9 +65,7 @@
         to_spectrum = jnp.einsum(
             "tlk,kcf->fctl", direction, dft_table, precision=lax.Precision.HIGHEST
         ).astype(jnp.bfloat16)
-        to_regrouped = lax.all_to_all(
-            to_spectrum, ("row", "col"), split_axis=0, concat_axis=3, tiled=True
-        )
+        to_regrouped = plan_the_gates(to_spectrum)
         spec_real = to_regrouped[:, 0]
         spec_imag = to_regrouped[:, 1]
         press_real = jnp.einsum(

time: 1140 us -> 1090 us (0.956)
  local copies, waits for them, and re-layouts: 250 us -> 203 us
    all_to_all x2 -> x0, local copies, waits for them, and re-layouts: 24.3 us -> none  [body(): lax.all_to_all(to_spectrum, ('row', 'col'), split_axis=0, concat_axis=3,...]
    convert_element_type x2 -> x0, local copies, waits for them, and re-layouts: 18.6 us -> none  [body(): to_spectrum = jnp.einsum('tlk,kcf->fctl', direction, dft_table, precision...]
    unnamed x34 -> x100, local copies, waits for them, and re-layouts: 112 us -> 103 us
where the time goes in v1:
time: 1090 us; the launch traced here: 1080 us
  matrix products  328 us (30%)
  blocking collectives  283 us (26%)
  local copies, waits for them, and re-layouts  203 us (19%)
  waiting for transfers between devices  155 us (14%)
  other arithmetic  93.1 us (9%)
  starting transfers between devices  11.5 us (1%)
    all_to_all x2, waiting for transfers between devices, to_taps(): lax.all_to_all(spectrum, ('row', 'col'), split_axis=3, concat_axis=0, til...  155 us
    all_to_all x2, blocking collectives, plan_the_gates(): newest = all_to_all(block_next, ('row', 'col'), 0, 0)  109 us
    unnamed x100, local copies, waits for them, and re-layouts  103 us
    all_to_all x1, blocking collectives, to_taps(): lax.all_to_all(spectrum, ('row', 'col'), split_axis=3, concat_axis=0, til...  98.5 us
    psum x2, blocking collectives, body(): lax.psum((along_term, jnp.sum(direction * image_taps)), ('row', 'col'))  75.5 us
    all_to_all x7, local copies, waits for them, and re-layouts, to_taps(): lax.all_to_all(spectrum, ('row', 'col'), split_axis=3, concat_axis=0, til...  58.6 us
    dot_general x3, matrix products, to_taps(): jnp.einsum('fctl,kcf->tlk', regrouped, dft_table, precision=lax.Precision...  57.9 us
    all_to_all x3, other arithmetic, to_taps(): lax.all_to_all(spectrum, ('row', 'col'), split_axis=3, concat_axis=0, til...  41.3 us
  transfers between devices with their start and end apart: 2, of which 2 were waited for; matrix products, arithmetic and copies ran while one was open for 3% of the time, Pallas kernels for 0%

profile of v1, /device:TPU:0, one launch (start us, length us, event | category | flops | bytes accessed | tf_op | source)
XLA Modules:
  0.0 1077.8 jit_solution(4105143637230933472)
XLA Ops:
  62.3 34.6 %sine_negate_fusion = (f32[1024,1,2048]{2,0,1:T(8,128)}, f32[1024,1,2048]{2,0,1:T(8,128)}) fusion(), kind=kLoop, calls=%fused_computation.57 | loop fusion | flops 31457280 | bytes 16777216 | tf_op jit(solution)/shard_map/neg | solution.py:26
  96.8 60.6 %all-to-all-done = f32[32,1,32768]{2,1,0:T(1,128)} async-done(((f32[32,1,32768]{2,1,0:T(1,128)}), f32[32,1,32768]{2,1,0:T(1,128)}, u32[]{:S(2)}, u32[]{:S(2)}) %all-to-all-start) | async-done | bytes 4194336 | tf_op jit(solution)/shard_map/all_to_all | solution.py:37
  158.0 13.8 %reduce = f32[32,32768]{1,0:T(8,128)} reduce(f32[32,1,32768]{2,1,0:T(1,128)} %all-to-all-done, f32[]{:T(128)} %broadcast.90), dimensions={1}, to_apply=%all_to_all.45.reduce_sub_computation | reduce | bytes 8388612 | tf_op jit(solution)/shard_map/all_to_all | solution.py:37
  198.4 18.7 %fusion.81 = f32[32,8,1024]{2,1,0:T(8,128)S(1)} fusion(f32[2048,2,32,8]{0,3,1,2:T(8,128)} %all_to_all.48, f32[1024,1,2048]{2,0,1:T(8,128)} %get-tuple-element.20, f32[1024,1,2048]{2,0,1:T(8,128)} %get-tuple-element.21), kind=kOutput, calls=%fused_computation.92 | convolution fusion | flops 12893290496 | bytes 22020096 | tf_op jit(solution)/shard_map/fctl,kcf->tlk/dot_general | solution.py:40
  218.0 19.9 %fusion.66 = bf16[2048,2,32,8]{0,2,3,1:T(8,128)(2,1)S(1)} fusion(f32[32,8,1024]{2,1,0:T(8,128)S(1)} %fusion.81, f32[1024,1,2048]{2,0,1:T(8,128)} %get-tuple-element.20, f32[1024,1,2048]{2,0,1:T(8,128)} %get-tuple-element.21), kind=kOutput, calls=%fused_computation.75 | convolution fusion | flops 12894339072 | bytes 19922944 | tf_op jit(solution)/shard_map/tlk,kcf->fctl/dot_general | solution.py:65
  249.6 52.7 %all_to_all.64 = bf16[32,2,16384]{2,1,0:T(2,128)(2,1)} all-to-all(bf16[32,2,16384]{2,1,0:T(2,128)(2,1)S(1)} %reshape.102), channel_id=1, replica_groups=mesh['row'=4,'col'=8] {'row','col'}, dimensions={0} | all-to-all | bytes 4194304 | tf_op jit(solution)/shard_map/all_to_all | solution.py:17
  319.9 12.7 %fusion.12 = f32[64,32,512]{2,1,0:T(8,128)} fusion(bf16[64,1,32,256]{3,2,0,1:T(8,128)(2,1)S(1)} %copy.83, bf16[64,2,512,256]{3,2,1,0:T(8,128)(2,1)} %param.6), kind=kOutput, calls=%fused_computation.13 | convolution fusion | flops 536870912 | bytes 22020096 | tf_op jit(solution)/shard_map/fml,ftl->ftm/dot_general | solution.py:80
  332.6 12.7 %fusion.34 = f32[64,32,512]{2,1,0:T(8,128)} fusion(bf16[64,1,32,256]{3,2,0,1:T(8,128)(2,1)S(1)} %copy.83, bf16[64,2,512,256]{3,2,1,0:T(8,128)(2,1)} %param.6), kind=kOutput, calls=%fused_computation.35 | convolution fusion | flops 536870912 | bytes 22020096 | tf_op jit(solution)/shard_map/fml,ftl->ftm/dot_general | solution.py:71
  348.4 12.7 %fusion.30 = f32[64,32,512]{2,1,0:T(8,128)} fusion(bf16[64,1,32,256]{3,2,0,1:T(8,128)(2,1)S(1)} %copy.84, bf16[64,2,512,256]{3,2,1,0:T(8,128)(2,1)} %param.6), kind=kOutput, calls=%fused_computation.31 | convolution fusion | flops 536870912 | bytes 22020096 | tf_op jit(solution)/shard_map/fml,ftl->ftm/dot_general | solution.py:77
  361.1 12.7 %fusion.14 = f32[64,32,512]{2,1,0:T(8,128)} fusion(bf16[64,1,32,256]{3,2,0,1:T(8,128)(2,1)S(1)} %copy.84, bf16[64,2,512,256]{3,2,1,0:T(8,128)(2,1)} %param.6), kind=kOutput, calls=%fused_computation.15 | convolution fusion | flops 536870912 | bytes 22020096 | tf_op jit(solution)/shard_map/fml,ftl->ftm/dot_general | solution.py:74
  373.8 11.9 %fusion.10 = f32[64,32,256]{2,1,0:T(8,128)} fusion(f32[64,32,512]{2,1,0:T(8,128)} %fusion.30, f32[64,32,512]{2,1,0:T(8,128)} %fusion.12, f32[32,512]{1,0:T(8,128)S(1)} %get-tuple-element.10, bf16[64,2,512,256]{3,2,1,0:T(8,128)(2,1)} %param.6), kind=kOutput, calls=%fused_computation.11 | convolution fusion | flops 540016640 | bytes 27328512 | tf_op jit(solution)/shard_map/fml,ftm->ftl/dot_general | solution.py:46
  385.8 11.9 %fusion.8 = f32[64,32,256]{2,1,0:T(8,128)} fusion(f32[64,32,512]{2,1,0:T(8,128)} %fusion.34, f32[64,32,512]{2,1,0:T(8,128)} %fusion.14, f32[32,512]{1,0:T(8,128)S(1)} %get-tuple-element.10, bf16[64,2,512,256]{3,2,1,0:T(8,128)(2,1)} %param.6), kind=kOutput, calls=%fused_computation.9 | convolution fusion | flops 540016640 | bytes 27328512 | tf_op jit(solution)/shard_map/fml,ftm->ftl/dot_general | solution.py:52
  397.7 12.8 %add_bitcast_fusion.3 = f32[64,1,32,256]{3,2,0,1:T(8,128)} fusion(f32[64,32,256]{2,1,0:T(8,128)} %fusion.10, f32[64,32,512]{2,1,0:T(8,128)} %fusion.34, f32[64,32,512]{2,1,0:T(8,128)} %fusion.14, f32[32,512]{1,0:T(8,128)S(1)} %get-tuple-element.10, bf16[64,1,32,256]{3,2,0,1:T(8,128)(2,1)S(1)} %copy.83, f32[64]{0:T(128)S(1)} %copy-done.11, ...), kind=kOutput, calls=%fused_computation.81 | convolution fusion | flops 542113792 | bytes 30474496 | tf_op jit(solution)/shard_map/fml,ftm->ftl/dot_general | solution.py:43
  410.5 13.1 %add_bitcast_fusion.2 = f32[64,1,32,256]{3,2,0,1:T(8,128)} fusion(f32[64,32,256]{2,1,0:T(8,128)} %fusion.8, f32[64,32,512]{2,1,0:T(8,128)} %fusion.30, f32[64,32,512]{2,1,0:T(8,128)} %fusion.12, f32[32,512]{1,0:T(8,128)S(1)} %get-tuple-element.10, bf16[64,1,32,256]{3,2,0,1:T(8,128)(2,1)S(1)} %copy.84, f32[64]{0:T(128)S(1)} %copy-done.11, ...), kind=kOutput, calls=%fused_computation.80 | convolution fusion | flops 542113792 | bytes 30474496 | tf_op jit(solution)/shard_map/fml,ftm->ftl/dot_general | solution.py:49
  450.8 94.5 %all-to-all-done.2 = f32[32,1,32768]{2,1,0:T(1,128)} async-done(((f32[32,1,32768]{2,1,0:T(1,128)}), f32[32,1,32768]{2,1,0:T(1,128)}, u32[]{:S(2)}, u32[]{:S(2)}) %all-to-all-start.2) | async-done | bytes 4194336 | tf_op jit(solution)/shard_map/all_to_all | solution.py:37
  545.3 13.8 %reduce.1 = f32[32,32768]{1,0:T(8,128)} reduce(f32[32,1,32768]{2,1,0:T(1,128)} %all-to-all-done.2, f32[]{:T(128)} %broadcast.90), dimensions={1}, to_apply=%all_to_all.50.reduce_sub_computation | reduce | bytes 8388612 | tf_op jit(solution)/shard_map/all_to_all | solution.py:37
  585.8 19.5 %multiply_reduce_fusion.2 = (f32[]{:T(128)}, f32[]{:T(128)}, f32[32,8,1024]{2,1,0:T(8,128)S(1)}) fusion(f32[32,8,1024]{2,1,0:T(8,128)S(1)} %copy-done.5, f32[2048,2,32,8]{0,3,1,2:T(8,128)} %all_to_all.53, f32[1024,1,2048]{2,0,1:T(8,128)} %get-tuple-element.20, f32[1024,1,2048]{2,0,1:T(8,128)} %get-tuple-element.21), kind=kOutput, calls=%fused_computation.113 | convolution fusion | flops 12894339072 | bytes 23068680 | tf_op jit(solution)/shard_map/fctl,kcf->tlk/dot_general | solution.py:40
  605.3 37.4 %all-reduce.1 = (f32[]{:T(128)}, f32[]{:T(128)}) all-reduce(f32[]{:T(128)} %get-tuple-element.5, f32[]{:T(128)} %get-tuple-element.4), channel_id=1, replica_groups=mesh['row'=4,'col'=8] {'row','col'}, use_global_device_ids=true, to_apply=%region_1.2 | all-reduce | flops 2 | bytes 16 | tf_op jit(solution)/shard_map/psum | solution.py:96
  644.3 20.3 %fusion.63 = bf16[2048,2,32,8]{0,2,3,1:T(8,128)(2,1)S(1)} fusion(f32[32,8,1024]{2,1,0:T(8,128)S(1)} %multiply_add_fusion.1, f32[1024,1,2048]{2,0,1:T(8,128)} %get-tuple-element.20, f32[1024,1,2048]{2,0,1:T(8,128)} %get-tuple-element.21), kind=kOutput, calls=%fused_computation.74 | convolution fusion | flops 12894339072 | bytes 19922944 | tf_op jit(solution)/shard_map/tlk,kcf->fctl/dot_general | solution.py:65
  676.3 55.8 %all_to_all.65 = bf16[32,2,16384]{2,1,0:T(2,128)(2,1)} all-to-all(bf16[32,2,16384]{2,1,0:T(2,128)(2,1)S(1)} %reshape.106), channel_id=1, replica_groups=mesh['row'=4,'col'=8] {'row','col'}, dimensions={0} | all-to-all | bytes 4194304 | tf_op jit(solution)/shard_map/all_to_all | solution.py:17
  749.7 12.7 %fusion.4 = f32[64,32,512]{2,1,0:T(8,128)} fusion(bf16[64,1,32,256]{3,2,0,1:T(8,128)(2,1)S(1)} %copy.85, bf16[64,2,512,256]{3,2,1,0:T(8,128)(2,1)} %param.6), kind=kOutput, calls=%fused_computation.5 | convolution fusion | flops 536870912 | bytes 22020096 | tf_op jit(solution)/shard_map/fml,ftl->ftm/dot_general | solution.py:80
  762.4 12.7 %fusion.26 = f32[64,32,512]{2,1,0:T(8,128)} fusion(bf16[64,1,32,256]{3,2,0,1:T(8,128)(2,1)S(1)} %copy.85, bf16[64,2,512,256]{3,2,1,0:T(8,128)(2,1)} %param.6), kind=kOutput, calls=%fused_computation.27 | convolution fusion | flops 536870912 | bytes 22020096 | tf_op jit(solution)/shard_map/fml,ftl->ftm/dot_general | solution.py:71
  778.0 12.7 %fusion.22 = f32[64,32,512]{2,1,0:T(8,128)} fusion(bf16[64,1,32,256]{3,2,0,1:T(8,128)(2,1)S(1)} %copy.86, bf16[64,2,512,256]{3,2,1,0:T(8,128)(2,1)} %param.6), kind=kOutput, calls=%fused_computation.23 | convolution fusion | flops 536870912 | bytes 22020096 | tf_op jit(solution)/shard_map/fml,ftl->ftm/dot_general | solution.py:77
  790.7 12.7 %fusion.6 = f32[64,32,512]{2,1,0:T(8,128)} fusion(bf16[64,1,32,256]{3,2,0,1:T(8,128)(2,1)S(1)} %copy.86, bf16[64,2,512,256]{3,2,1,0:T(8,128)(2,1)} %param.6), kind=kOutput, calls=%fused_computation.7 | convolution fusion | flops 536870912 | bytes 22020096 | tf_op jit(solution)/shard_map/fml,ftl->ftm/dot_general | solution.py:74
  803.4 11.9 %fusion.2 = f32[64,32,256]{2,1,0:T(8,128)} fusion(f32[64,32,512]{2,1,0:T(8,128)} %fusion.22, f32[64,32,512]{2,1,0:T(8,128)} %fusion.4, f32[32,512]{1,0:T(8,128)S(1)} %get-tuple-element.10, bf16[64,2,512,256]{3,2,1,0:T(8,128)(2,1)} %param.6), kind=kOutput, calls=%fused_computation.3 | convolution fusion | flops 540016640 | bytes 27328512 | tf_op jit(solution)/shard_map/fml,ftm->ftl/dot_general | solution.py:46
  815.3 11.9 %fusion = f32[64,32,256]{2,1,0:T(8,128)} fusion(f32[64,32,512]{2,1,0:T(8,128)} %fusion.26, f32[64,32,512]{2,1,0:T(8,128)} %fusion.6, f32[32,512]{1,0:T(8,128)S(1)} %get-tuple-element.10, bf16[64,2,512,256]{3,2,1,0:T(8,128)(2,1)} %param.6), kind=kOutput, calls=%fused_computation.1 | convolution fusion | flops 540016640 | bytes 27328512 | tf_op jit(solution)/shard_map/fml,ftm->ftl/dot_general | solution.py:52
  827.2 12.8 %add_bitcast_fusion.1 = f32[64,1,32,256]{3,2,0,1:T(8,128)} fusion(f32[64,32,256]{2,1,0:T(8,128)} %fusion.2, f32[64,32,512]{2,1,0:T(8,128)} %fusion.26, f32[64,32,512]{2,1,0:T(8,128)} %fusion.6, f32[32,512]{1,0:T(8,128)S(1)} %get-tuple-element.10, bf16[64,1,32,256]{3,2,0,1:T(8,128)(2,1)S(1)} %copy.85, f32[64]{0:T(128)S(1)} %copy-done.11, ...), kind=kOutput, calls=%fused_computation.79 | convolution fusion | flops 542113792 | bytes 30474496 | tf_op jit(solution)/shard_map/fml,ftm->ftl/dot_general | solution.py:43
  840.0 13.1 %add_bitcast_fusion = f32[64,1,32,256]{3,2,0,1:T(8,128)} fusion(f32[64,32,256]{2,1,0:T(8,128)} %fusion, f32[64,32,512]{2,1,0:T(8,128)} %fusion.22, f32[64,32,512]{2,1,0:T(8,128)} %fusion.4, f32[32,512]{1,0:T(8,128)S(1)} %get-tuple-element.10, bf16[64,1,32,256]{3,2,0,1:T(8,128)(2,1)S(1)} %copy.86, f32[64]{0:T(128)S(1)} %copy-done.11, ...), kind=kOutput, calls=%fused_computation.78 | convolution fusion | flops 542113792 | bytes 30474496 | tf_op jit(solution)/shard_map/fml,ftm->ftl/dot_general | solution.py:49
  876.2 98.5 %all_to_all.66 = f32[32,1,32768]{2,1,0:T(1,128)} all-to-all(f32[32,1,32768]{2,1,0:T(1,128)} %reshape.108), channel_id=1, replica_groups=mesh['row'=4,'col'=8] {'row','col'}, dimensions={0} | all-to-all | bytes 8388608 | tf_op jit(solution)/shard_map/all_to_all | solution.py:37
  974.7 13.8 %reduce.2 = f32[32,32768]{1,0:T(8,128)} reduce(f32[32,1,32768]{2,1,0:T(1,128)} %all_to_all.66, f32[]{:T(128)} %broadcast.90), dimensions={1}, to_apply=%all_to_all.55.reduce_sub_computation | reduce | bytes 8388612 | tf_op jit(solution)/shard_map/all_to_all | solution.py:37
  1015.3 19.6 %multiply_reduce_fusion = (f32[]{:T(128)}, f32[]{:T(128)}, f32[32,8,1024]{2,1,0:T(8,128)}) fusion(f32[32,8,1024]{2,1,0:T(8,128)S(1)} %copy-done.10, f32[32,8,1024]{2,1,0:T(8,128)S(1)} %copy-done.6, f32[32,8,1024]{2,1,0:T(8,128)S(1)} %copy-done.8, f32[]{:T(128)S(6)} %div.14, f32[2048,2,32,8]{0,3,1,2:T(8,128)} %all_to_all.58, ...), kind=kOutput, calls=%fused_computation.109 | convolution fusion | flops 12894863360 | bytes 25165836 | tf_op jit(solution)/shard_map/fctl,kcf->tlk/dot_general | solution.py:40
  1034.9 38.1 %all-reduce = (f32[]{:T(128)}, f32[]{:T(128)}) all-reduce(f32[]{:T(128)} %get-tuple-element.3, f32[]{:T(128)} %get-tuple-element.2), channel_id=1, replica_groups=mesh['row'=4,'col'=8] {'row','col'}, use_global_device_ids=true, to_apply=%region_5.6 | all-reduce | flops 2 | bytes 16 | tf_op jit(solution)/shard_map/psum | solution.py:96
  (131 shorter events, 260.5 us)
Async XLA Ops:
  54.3 103.1 %all-to-all-start = ((f32[32,1,32768]{2,1,0:T(1,128)}), f32[32,1,32768]{2,1,0:T(1,128)}, u32[]{:S(2)}, u32[]{:S(2)}) async-start(f32[32,1,32768]{2,1,0:T(1,128)} %reshape.100), calls=%async_computation | async-start | bytes 8388608 | tf_op jit(solution)/shard_map/all_to_all | solution.py:37
  217.1 1.0 copy-start.4
  240.8 1.9 copy-start.2
  385.8 11.9 %copy-start.11 = (f32[64]{0:T(128)S(1)}, f32[64]{0:T(128)}, u32[]{:S(2)}) copy-start(f32[64]{0:T(128)} %param.10) | copy-start | bytes 772
  410.5 13.1 %copy-start.1 = (f32[64,1,32,256]{3,2,0,1:T(8,128)S(1)}, f32[64,1,32,256]{3,2,0,1:T(8,128)}, u32[]{:S(2)}) copy-start(f32[64,1,32,256]{3,2,0,1:T(8,128)} %add_bitcast_fusion.3) | copy-start | bytes 6291460
  446.6 98.7 %all-to-all-start.2 = ((f32[32,1,32768]{2,1,0:T(1,128)}), f32[32,1,32768]{2,1,0:T(1,128)}, u32[]{:S(2)}, u32[]{:S(2)}) async-start(f32[32,1,32768]{2,1,0:T(1,128)} %reshape.104), calls=%async_computation.2 | async-start | bytes 8388608 | tf_op jit(solution)/shard_map/all_to_all | solution.py:37
  577.8 7.9 copy-start.5
  605.3 59.3 %copy-start.7 = (f32[32,8,1024]{2,1,0:T(8,128)}, f32[32,8,1024]{2,1,0:T(8,128)S(1)}, u32[]{:S(2)}) copy-start(f32[32,8,1024]{2,1,0:T(8,128)S(1)} %get-tuple-element.18) | copy-start | bytes 3145732
  644.3 20.3 %copy-start.9 = (f32[32,8,1024]{2,1,0:T(8,128)}, f32[32,8,1024]{2,1,0:T(8,128)S(1)}, u32[]{:S(2)}) copy-start(f32[32,8,1024]{2,1,0:T(8,128)S(1)} %multiply_add_fusion.1) | copy-start | bytes 3145732
  667.5 1.9 copy-start.3
  840.0 13.1 %copy-start = (f32[64,1,32,256]{3,2,0,1:T(8,128)S(1)}, f32[64,1,32,256]{3,2,0,1:T(8,128)}, u32[]{:S(2)}) copy-start(f32[64,1,32,256]{3,2,0,1:T(8,128)} %add_bitcast_fusion.1) | copy-start | bytes 6291460
  1007.3 8.0 copy-start.6
  1007.3 8.0 copy-start.8
  1007.3 8.0 copy-start.10
